TPU v7x, 512 devices: a whole 4x4x16 slice. The times are simulated.
512 devices in a mesh: feat: 32 (over x, y, core), rep: 16 (over z).
Axes of the slice: x: 4, y: 4, z: 16, core: 2. Of those that a mesh axis runs over, the one named last changes fastest.
Arguments:
- feats: bfloat16 [16, 8192, 1024], P('rep', None, 'feat'), may hold values from -6 to 6
- w_self: bfloat16 [1024, 256], P('feat'), may hold values from -0.1875 to 0.1875
- w_neigh: bfloat16 [1024, 256], P('feat'), may hold values from -0.1875 to 0.1875
- bias: float32 [256], replicated, may hold values from -3 to 3
- tile_weight: bfloat16 [16, 32, 3, 128, 128], P('rep'), may hold values from -0.375 to 0.375
- tile_src: int32 [16, 32, 3], P('rep'), may hold values from 0 to 63
- tile_count: int32 [16, 32], P('rep'), may hold values from 1 to 3
- owner_order: int32 [16, 32], P('rep'), may hold values from 0 to 31, each once within a row
- cotangent: bfloat16 [16, 4096, 256], P('rep', 'feat'), may hold values from -6 to 6
Outputs:
- hidden: bfloat16 [16, 4096, 256], P('rep', 'feat')
- grad_self: float32 [1024, 256], P('feat')
- grad_neigh: float32 [1024, 256], P('feat')
All inputs are finite; a program needn't handle non-finite values.
Results may differ from a plain program's by a relative error of at most 0.0055.
Values may be sent and summed in bfloat16 or wider, within the bound.
A program may use at most 64 MiB of HBM per device.

v0:
```python
import jax
import jax.numpy as jnp
from jax import lax
from jax.sharding import PartitionSpec as P


def transposed_product(left, right):
    return lax.dot_general(
        left, right, (((0,), (0,)), ((), ())), preferred_element_type=jnp.float32
    )


def body(feats, w_self, w_neigh, bias, tile_weight, tile_src, tile_count, owner_order, cotangent):
    block_rows = tile_weight.shape[3]
    tile_slots = tile_weight.shape[2]
    columns = feats.shape[2]
    by_block = feats[0].reshape(-1, block_rows, columns)
    in_use = jnp.arange(tile_slots)[None, :] < tile_count[0][:, None]
    masked = jnp.where(in_use[:, :, None, None], tile_weight[0], jnp.zeros((), jnp.bfloat16))
    sources = by_block[tile_src[0]]
    aggregate = jnp.einsum(
        "bkij,bkjc->bic", masked, sources, preferred_element_type=jnp.float32
    ).astype(jnp.bfloat16)
    target_rows = by_block[owner_order[0]].reshape(-1, columns)
    target_mean = aggregate[owner_order[0]].reshape(-1, columns)
    partial_sums = jnp.dot(target_rows, w_self, preferred_element_type=jnp.float32)
    partial_sums = partial_sums + jnp.dot(target_mean, w_neigh, preferred_element_type=jnp.float32)
    preact = lax.psum_scatter(partial_sums, "feat", scatter_dimension=0, tiled=True) + bias
    hidden = jax.nn.silu(preact).astype(jnp.bfloat16)
    squash = jax.nn.sigmoid(preact)
    output_grad = (
        cotangent[0].astype(jnp.float32) * squash * (1.0 + preact * (1.0 - squash))
    ).astype(jnp.bfloat16)
    pieces = lax.all_gather(output_grad, "feat", axis=0, tiled=True)
    grad_self = transposed_product(target_rows, pieces)
    grad_neigh = transposed_product(target_mean, pieces)
    grad_self, grad_neigh = lax.psum((grad_self, grad_neigh), "rep")
    return (hidden[None], grad_self, grad_neigh)


def solution(mesh):
    in_specs = (
        P("rep", None, "feat"),
        P("feat", None),
        P("feat", None),
        P(),
        P("rep", None, None, None, None),
        P("rep", None, None),
        P("rep", None),
        P("rep", None),
        P("rep", "feat", None),
    )
    out_specs = (P("rep", "feat", None), P("feat", None), P("feat", None))
    return jax.shard_map(body, mesh=mesh, in_specs=in_specs, out_specs=out_specs, check_vma=False)
```

profile of v0, /device:TPU:2, one launch (start us, length us, event | category | flops | bytes accessed | tf_op | source)
XLA Modules:
  0.0 341.3 jit_solution(3312335809542064258)
XLA Ops:
  7.2 0.0 copy-start
  7.2 0.0 reduce-scatter.2.cloned.1.call-start
  7.2 0.7 fusion.20
  7.9 0.7 compare_select_fusion
  8.6 0.7 iota_compare_fusion
  9.3 0.1 copy.18
  9.4 0.1 reshape.130
  9.5 1.2 copy.24
  10.7 0.3 copy.16
  11.0 0.6 gather_fusion
  11.6 0.7 gather_fusion.1
  12.4 3.2 fusion.4
  15.5 0.0 copy-start.2
  15.6 0.6 gather_fusion.2
  16.2 0.0 copy-done
  16.2 0.7 fusion.10
  16.9 0.0 copy-done.2
  16.9 2.7 convolution_add_fusion
  19.6 0.0 reduce-scatter.2.cloned.1.call-update
  19.7 0.0 all-gather.2.cloned.1.call-start
  19.7 109.6 %reduce-scatter.2.cloned.1.call-done = f32[128,256]{1,0:T(8,128)} async-done(((f32[4096,256]{1,0:T(8,128)}), f32[128,256]{1,0:T(8,128)}) %reduce-scatter.2.cloned.1.call-update) | async-done | bytes 131088 | tf_op jit(solution)/shard_map/reduce_scatter | solution.py:28
  129.4 0.0 copy-done.1
  129.4 1.6 fusion.17
  131.0 0.0 all-gather.2.cloned.1.call-update
  131.0 0.0 all-reduce.3.cloned.1.call-start
  131.0 59.8 %all-gather.2.cloned.1.call-done = bf16[4096,256]{1,0:T(8,128)(2,1)} async-done(((bf16[128,256]{1,0:T(8,128)(2,1)}), bf16[4096,256]{1,0:T(8,128)(2,1)}) %all-gather.2.cloned.1.call-update) | async-done | bytes 2097168 | tf_op jit(solution)/shard_map/all_gather | solution.py:34
  190.8 2.7 fusion.5
  193.5 2.7 fusion.8
  196.2 0.0 all-reduce.3.cloned.1.call-update
  196.2 135.8 %all-reduce.3.cloned.1.call-done = (f32[32,256]{1,0:T(8,128)}, f32[32,256]{1,0:T(8,128)}) async-done(((f32[32,256]{1,0:T(8,128)}, f32[32,256]{1,0:T(8,128)}), (f32[32,256]{1,0:T(8,128)}, f32[32,256]{1,0:T(8,128)})) %all-reduce.3.cloned.1.call-update) | async-done | bytes 65552 | tf_op jit(solution)/shard_map/psum | solution.py:37
  332.0 1.4 copy.43
  333.4 1.4 copy.44
  (5 shorter events, 0.0 us)
Async XLA Ops:
  7.2 9.0 %copy-start = (bf16[32,256]{1,0:T(8,128)(2,1)S(1)}, bf16[32,256]{1,0:T(8,128)(2,1)}, u32[]{:S(2)}) copy-start(bf16[32,256]{1,0:T(8,128)(2,1)} %param.10) | copy-start | bytes 49156
  7.2 122.2 %reduce-scatter.2.cloned.1.call-start = ((), (), s32[]{:S(2)}) async-start(), calls=%async_computation.1 | async-start | bytes 4325376 | tf_op jit(solution)/shard_map/reduce_scatter | solution.py:28
  15.5 1.4 copy-start.2
  19.6 109.7 %copy-start.1 = (bf16[1,128,256]{2,1,0:T(8,128)(2,1)S(1)}, bf16[1,128,256]{2,1,0:T(8,128)(2,1)}, u32[]{:S(2)}) copy-start(bf16[1,128,256]{2,1,0:T(8,128)(2,1)} %param.17) | copy-start | bytes 196612
  19.6 109.7 %copy-start.3 = (f32[256]{0:T(256)S(1)}, f32[256]{0:T(256)}, u32[]{:S(2)}) copy-start(f32[256]{0:T(256)} %param.12) | copy-start | bytes 3076
  19.7 171.2 %all-gather.2.cloned.1.call-start = ((), (), s32[]{:S(2)}) async-start(), calls=%async_computation.2 | async-start | bytes 2162688 | tf_op jit(solution)/shard_map/all_gather | solution.py:34
  131.0 201.0 %all-reduce.3.cloned.1.call-start = ((), (), s32[]{:S(2)}) async-start(), calls=%async_computation.3 | async-start | bytes 131072 | tf_op jit(solution)/shard_map/psum | solution.py:37
Sparse Core Ops, SparseCore 0:
  19.8 109.5 reduce-scatter.1
  132.5 58.3 all-gather.1
  196.3 135.6 all-reduce.2
where the time goes:
time: 342 us; the launch traced here: 341 us
  waiting for transfers between devices  305 us (89%)
  between operations  13.8 us (4%)
  matrix products  11.9 us (3%)
  local copies, waits for them, and re-layouts  6.39 us (2%)
  other arithmetic  3.69 us (1%)
    psum x1, waiting for transfers between devices, body(): grad_self, grad_neigh = lax.psum((grad_self, grad_neigh), 'rep')  136 us
    reduce_scatter x1, waiting for transfers between devices, body(): lax.psum_scatter(partial_sums, 'feat', scatter_dimension=0, tiled=True)  110 us
    all_gather x1, waiting for transfers between devices, body(): pieces = lax.all_gather(output_grad, 'feat', axis=0, tiled=True)  59.8 us
  transfers between devices with their start and end apart: 3, of which 3 were waited for; matrix products, arithmetic and copies ran while one was open for 0% of the time, Pallas kernels for 0%

commit v1 on v0

v1 whole, which is shorter than its diff:
```python
import functools

import jax
import jax.numpy as jnp
from jax import lax
from jax.experimental import pallas as pl
from jax.experimental.pallas import tpu as pltpu
from jax.sharding import PartitionSpec as P

MESH = pl.DeviceIdType.MESH
SIDE = 4
PLANE = 2 * SIDE * SIDE
F32 = jnp.float32
BF16 = jnp.bfloat16


def remote(src, dst, send_sem, recv_sem, axis, index):
    return pltpu.make_async_remote_copy(
        src_ref=src,
        dst_ref=dst,
        send_sem=send_sem,
        recv_sem=recv_sem,
        device_id={axis: index},
        device_id_type=MESH,
    )


def exchange_kernel(
    reps,
    slots,
    src_ref,
    count_ref,
    order_ref,
    feats_hbm,
    tiles_hbm,
    w_self_hbm,
    w_neigh_hbm,
    bias_ref,
    cot_ref,
    hidden_ref,
    total_ref,
    feats,
    tiles,
    mine,
    rows,
    weights,
    grads,
    part,
    parts,
    load_sems,
    a2a_send,
    a2a_recv,
    w_send,
    w_recv,
    g_send,
    g_recv,
    z_send,
    z_recv,
    t_send,
    t_recv,
):
    me = lax.axis_index("feat")
    z = lax.axis_index("rep")
    x, y, c = me // (2 * SIDE), (me // 2) % SIDE, me % 2

    loads = [
        pltpu.make_async_copy(w_self_hbm, weights.at[0, pl.ds(0, 32)], load_sems.at[0]),
        pltpu.make_async_copy(w_neigh_hbm, weights.at[0, pl.ds(32, 32)], load_sems.at[1]),
        pltpu.make_async_copy(tiles_hbm, tiles, load_sems.at[2]),
    ]
    for load in loads:
        load.start()

    def load_block(s, carry):
        lanes = pl.ds(pl.multiple_of(s * 128, 128), 128)
        pltpu.make_async_copy(feats_hbm.at[:, lanes], feats.at[s], load_sems.at[3]).start()
        return carry

    lax.fori_loop(0, feats.shape[0], load_block, 0)

    barrier = pltpu.get_barrier_semaphore()

    def greet_plane(d, carry):
        pl.semaphore_signal(
            barrier, inc=1, device_id={"feat": lax.rem(me + d, PLANE)}, device_id_type=MESH
        )
        return carry

    def greet_rep(d, carry):
        pl.semaphore_signal(
            barrier, inc=1, device_id={"rep": lax.rem(z + d, reps)}, device_id_type=MESH
        )
        return carry

    lax.fori_loop(1, reps, greet_rep, 0)
    lax.fori_loop(1, PLANE, greet_plane, 0)

    for load in loads:
        load.wait()
    pltpu.make_async_copy(feats, feats, load_sems.at[3]).wait()

    def combine(p, carry):
        block = order_ref[0, p]
        used = count_ref[0, block]
        total = jnp.zeros((32, 128), F32)
        for k in range(slots):
            product = lax.dot_general(
                feats[src_ref[k, block]],
                tiles[block, k],
                (((1,), (1,)), ((), ())),
                preferred_element_type=F32,
            )
            total = total + product * (k < used).astype(F32)
        mine[p, 0:32, :] = feats[block]
        mine[p, 32:64, :] = total.astype(BF16)
        return carry

    lax.fori_loop(0, PLANE, combine, 0)
    pl.semaphore_wait(barrier, PLANE + reps - 2)

    def at(dx, dy, dc):
        return (
            lax.rem(x + dx, SIDE) * (2 * SIDE) + lax.rem(y + dy, SIDE) * 2 + lax.rem(c + dc, 2)
        )

    first = lambda k: (k * (1 - c) * SIDE + k * c) * 2
    second = lambda k: (k * c * SIDE + k * (1 - c)) * 2
    first_at = lambda k: at(k * (1 - c), k * c, 0)
    second_at = lambda k: at(k * c, k * (1 - c), 0)
    partner = at(0, 0, 1)

    class Gather:
        def __init__(self, buffer, send, recv):
            self.buffer, self.send, self.recv = buffer, send, recv
            self.sent = []

        def go(self, source, target, index):
            copy = remote(
                self.buffer.at[source],
                self.buffer.at[target],
                self.send.at[len(self.sent)],
                self.recv.at[target],
                "feat",
                index,
            )
            copy.start()
            self.sent.append(copy)

        def got(self, slot):
            remote(
                self.buffer.at[slot],
                self.buffer.at[slot],
                self.send.at[0],
                self.recv.at[slot],
                "feat",
                partner,
            ).wait_recv()

        def stage_one(self):
            for k in (1, 3, 2):
                self.go(0, first(k), first_at(k))
                self.go(0, second(k), second_at(k))
            self.go(0, 1, partner)

        def stage_two(self):
            for k in (1, 3, 2):
                self.got(first(k))
                for j in (1, 3, 2):
                    self.go(first(k), first(k) + second(j), second_at(j))
                self.go(first(k), first(k) + 1, partner)
            for k in (1, 3, 2):
                self.got(second(k))
                self.go(second(k), second(k) + 1, partner)

        def stage_three(self):
            for k in (1, 3, 2):
                for j in (1, 3, 2):
                    self.got(first(k) + second(j))
                    self.go(first(k) + second(j), first(k) + second(j) + 1, partner)

        def finish(self):
            for s in range(SIDE * SIDE):
                self.got(2 * s + 1)

        def drain(self):
            for copy in self.sent:
                copy.wait_send()

    w_gather = Gather(weights, w_send, w_recv)
    w_gather.stage_one()

    rows[0] = mine[me]

    def send_rows(d, carry):
        dx, dy, dc = d // (2 * SIDE), (d // 2) % SIDE, d % 2
        target = at(dx, dy, dc)
        remote(mine.at[target], rows.at[d], a2a_send, a2a_recv, "feat", target).start()
        return carry

    lax.fori_loop(1, PLANE, send_rows, 0)
    w_gather.stage_two()
    w_gather.stage_three()
    w_gather.finish()
    every = pl.ds(1, PLANE - 1)
    all_rows = remote(rows.at[every], rows.at[every], a2a_send, a2a_recv, "feat", partner)
    all_rows.wait_recv()

    def forward(g, acc):
        left = rows[pl.ds(4 * g, 4)].reshape(256, 128)
        right = weights[pl.ds(4 * g, 4)].reshape(256, 256)
        return acc + lax.dot_general(
            left, right, (((0,), (0,)), ((), ())), preferred_element_type=F32
        )

    preact = lax.fori_loop(0, PLANE // 4, forward, jnp.zeros((128, 256), F32)) + bias_ref[...]
    squash = jax.nn.sigmoid(preact)
    hidden_ref[...] = (preact * squash).astype(BF16)
    grads[0] = (cot_ref[...].astype(F32) * squash * (1.0 + preact * (1.0 - squash))).astype(BF16)

    g_gather = Gather(grads, g_send, g_recv)
    g_gather.stage_one()
    g_gather.stage_two()
    g_gather.stage_three()
    g_gather.finish()

    def backward(s, acc):
        px = lax.rem(x + SIDE - s // SIDE, SIDE)
        py = lax.rem(y + SIDE - s % SIDE, SIDE)
        base = px * (2 * SIDE) + py * 2
        left = jnp.concatenate([mine[base + c], mine[base + 1 - c]], axis=1)
        right = grads[pl.ds(2 * s, 2)].reshape(256, 256)
        return acc + jnp.dot(left, right, preferred_element_type=F32)

    grad = lax.fori_loop(0, SIDE * SIDE, backward, jnp.zeros((64, 256), F32))
    for row in range(8):
        for col in range(2):
            part[row * 2 + col] = grad[row * 8 : row * 8 + 8, col * 128 : col * 128 + 128]

    def scatter(d, carry):
        target = lax.rem(z + d, reps)
        remote(part.at[target], parts.at[d], z_send, z_recv, "rep", target).start()
        return carry

    lax.fori_loop(1, reps, scatter, 0)
    parts[0] = part[z]
    others = pl.ds(1, reps - 1)
    all_parts = remote(parts.at[others], parts.at[others], z_send, z_recv, "rep", 0)
    all_parts.wait_recv()

    acc = parts[0]
    for d in range(1, reps):
        acc = acc + parts[d]
    total_ref[0] = acc

    def spread(d, carry):
        target = lax.rem(z + d, reps)
        remote(total_ref.at[0], total_ref.at[d], t_send, t_recv, "rep", target).start()
        return carry

    lax.fori_loop(1, reps, spread, 0)
    all_total = remote(total_ref.at[others], total_ref.at[others], t_send, t_recv, "rep", 0)
    all_total.wait_recv()
    all_total.wait_send()
    all_parts.wait_send()
    all_rows.wait_send()
    w_gather.drain()
    g_gather.drain()


def finish_kernel(reps, hidden_in, total_in, hidden_ref, grad_self_ref, grad_neigh_ref):
    z = lax.axis_index("rep")
    hidden_ref[0] = hidden_in[...]
    for piece in range(16):
        row, col = piece // 2, piece % 2
        value = total_in[lax.rem(z + reps - piece, reps)]
        target = grad_self_ref if row < 4 else grad_neigh_ref
        target[row % 4 * 8 : row % 4 * 8 + 8, col * 128 : col * 128 + 128] = value


def solution(mesh):
    reps = mesh.shape["rep"]

    def body(feats, w_self, w_neigh, bias, tile_weight, tile_src, tile_count, owner_order, cotangent):
        slots = tile_weight.shape[2]
        smem = pl.BlockSpec(memory_space=pltpu.SMEM)
        vmem = pl.BlockSpec(memory_space=pltpu.VMEM)
        anywhere = pl.BlockSpec(memory_space=pl.ANY)
        dma = pltpu.SemaphoreType.DMA
        hidden, total = pl.pallas_call(
            functools.partial(exchange_kernel, reps, slots),
            out_shape=(
                jax.ShapeDtypeStruct((128, 256), BF16),
                jax.ShapeDtypeStruct((reps, 8, 128), F32),
            ),
            in_specs=[smem] * 3 + [anywhere] * 4 + [vmem] * 2,
            out_specs=(vmem, vmem),
            scratch_shapes=[
                pltpu.VMEM((64, 32, 128), BF16),
                pltpu.VMEM((32, slots, 128, 128), BF16),
                pltpu.VMEM((PLANE, 64, 128), BF16),
                pltpu.VMEM((PLANE, 64, 128), BF16),
                pltpu.VMEM((PLANE, 64, 256), BF16),
                pltpu.VMEM((PLANE, 128, 256), BF16),
                pltpu.VMEM((reps, 8, 128), F32),
                pltpu.VMEM((reps, 8, 128), F32),
                dma((4,)),
                dma,
                dma,
                dma((PLANE,)),
                dma((PLANE,)),
                dma((PLANE,)),
                dma((PLANE,)),
                dma,
                dma,
                dma,
                dma,
            ],
            compiler_params=pltpu.CompilerParams(collective_id=0, has_side_effects=True),
            name="exchange",
        )(
            tile_src[0].T,
            tile_count,
            owner_order,
            feats[0].T,
            tile_weight[0],
            w_self,
            w_neigh,
            bias.reshape(1, -1),
            cotangent[0],
        )
        return pl.pallas_call(
            functools.partial(finish_kernel, reps),
            out_shape=(
                jax.ShapeDtypeStruct((1, 128, 256), BF16),
                jax.ShapeDtypeStruct((32, 256), F32),
                jax.ShapeDtypeStruct((32, 256), F32),
            ),
            in_specs=[vmem] * 2,
            out_specs=(vmem,) * 3,
            name="finish",
        )(hidden, total)

    in_specs = (
        P("rep", None, "feat"),
        P("feat", None),
        P("feat", None),
        P(),
        P("rep", None, None, None, None),
        P("rep", None, None),
        P("rep", None),
        P("rep", None),
        P("rep", "feat", None),
    )
    out_specs = (P("rep", "feat", None), P("feat", None), P("feat", None))
    return jax.shard_map(body, mesh=mesh, in_specs=in_specs, out_specs=out_specs, check_vma=False)
```

time: 342 us -> 68.9 us (0.20)
  the two profiles are of different devices: /device:TPU:2 before, /device:TPU:1 now
where the time goes in v1:
time: 68.9 us; the launch traced here: 68.6 us
  Pallas kernels  66.7 us (97%)
  local copies, waits for them, and re-layouts  1.26 us (2%)
    pallas_call x1, Pallas kernels, body(): pl.pallas_call(functools.partial(exchange_kernel, reps, slots), out_shape...  65.2 us
    pallas_call x1, Pallas kernels, body(): pl.pallas_call(functools.partial(finish_kernel, reps), out_shape=(jax.Sha...  1.53 us

profile of v1, /device:TPU:1, one launch (start us, length us, event | category | flops | bytes accessed | tf_op | source)
XLA Modules:
  0.0 68.6 jit_solution(3544385056548679787)
XLA Ops:
  0.6 1.3 %copy.14 = s32[1,32,3]{1,2,0:T(4,128)} copy(s32[1,32,3]{1,0,2:T(1,128)} %param.14) | data formatting | bytes 768
  1.9 65.2 %exchange.1 = (bf16[128,256]{1,0:T(8,128)(2,1)}, f32[16,8,128]{2,1,0:T(8,128)}) custom-call(s32[3,32]{1,0:T(4,128)} %bitcast.14, s32[1,32]{1,0:T(1,128)} %count_ref.1, s32[1,32]{1,0:T(1,128)} %order_ref.1, bf16[32,8192]{1,0:T(8,128)(2,1)} %bitcast.12, bf16[32,3,128,128]{3,2,1,0:T(8,128)(2,1)} %bitcast.11, bf16[32,256]{1,0:T(8,128)(2,1)} %w_self_hbm.1, ...), custom_call_target="tpu_custom_call" | custom-call | tf_op jit(solution)/shard_map/exchange/pallas_call | solution.py:289
  67.1 1.5 %finish.1 = (bf16[1,128,256]{2,1,0:T(8,128)(2,1)}, f32[32,256]{1,0:T(8,128)}, f32[32,256]{1,0:T(8,128)}) custom-call(bf16[128,256]{1,0:T(8,128)(2,1)} %get-tuple-element.5.hidden_in, f32[16,8,128]{2,1,0:T(8,128)} %get-tuple-element.6.total_in), custom_call_target="tpu_custom_call" | custom-call | tf_op jit(solution)/shard_map/finish/pallas_call | solution.py:331

commit v2 on v1

v2 whole, which is shorter than its diff:
```python
import functools

import jax
import jax.numpy as jnp
from jax import lax
from jax.experimental import pallas as pl
from jax.experimental.pallas import tpu as pltpu
from jax.sharding import PartitionSpec as P

MESH = pl.DeviceIdType.MESH
SIDE = 4
PLANE = 2 * SIDE * SIDE
F32 = jnp.float32
BF16 = jnp.bfloat16


def remote(src, dst, send_sem, recv_sem, axis, index):
    return pltpu.make_async_remote_copy(
        src_ref=src,
        dst_ref=dst,
        send_sem=send_sem,
        recv_sem=recv_sem,
        device_id={axis: index},
        device_id_type=MESH,
    )


def exchange_kernel(
    reps,
    slots,
    src_ref,
    count_ref,
    order_ref,
    feats_hbm,
    tiles_hbm,
    w_self_hbm,
    w_neigh_hbm,
    bias_hbm,
    cot_hbm,
    hidden_out,
    total_out,
    feats,
    tiles,
    means,
    mine,
    rows,
    weights,
    grads,
    cot,
    bias,
    hidden,
    part,
    near,
    far,
    whole,
    load_sems,
    tile_sems,
    out_sems,
    ready_sems,
    a2a_send,
    a2a_recv,
    w_send,
    w_recv,
    g_send,
    g_recv,
    z_send,
    z_recv,
):
    me = lax.axis_index("feat")
    z = lax.axis_index("rep")
    x, y, c = me // (2 * SIDE), (me // 2) % SIDE, me % 2
    blocks = tiles.shape[0]
    chunks = tile_sems.shape[0]
    chunk = blocks // chunks

    barrier = pltpu.get_barrier_semaphore()

    def greet_plane(d, carry):
        pl.semaphore_signal(
            barrier, inc=1, device_id={"feat": lax.rem(me + d, PLANE)}, device_id_type=MESH
        )
        return carry

    lax.fori_loop(1, PLANE, greet_plane, 0)
    for d in range(1, 5):
        for target in (lax.rem(z + d, reps), lax.rem(z + reps - d, reps)):
            pl.semaphore_signal(barrier, inc=1, device_id={"rep": target}, device_id_type=MESH)

    w_loads = [
        pltpu.make_async_copy(w_self_hbm, weights.at[0, pl.ds(0, 32)], load_sems.at[0]),
        pltpu.make_async_copy(w_neigh_hbm, weights.at[0, pl.ds(32, 32)], load_sems.at[1]),
    ]
    for load in w_loads:
        load.start()

    def load_block(s, carry):
        lanes = pl.ds(pl.multiple_of(s * 128, 128), 128)
        pltpu.make_async_copy(feats_hbm.at[:, lanes], feats.at[s], load_sems.at[2]).start()
        return carry

    lax.fori_loop(0, feats.shape[0], load_block, 0)
    tile_loads = []
    for i in range(chunks):
        piece = pl.ds(i * chunk, chunk)
        tile_loads.append(pltpu.make_async_copy(tiles_hbm.at[piece], tiles.at[piece], tile_sems.at[i]))
        tile_loads[-1].start()
    small_loads = [
        pltpu.make_async_copy(bias_hbm, bias, load_sems.at[3]),
        pltpu.make_async_copy(cot_hbm, cot, load_sems.at[4]),
    ]
    for load in small_loads:
        load.start()

    def at(dx, dy, dc):
        return (
            lax.rem(x + dx, SIDE) * (2 * SIDE) + lax.rem(y + dy, SIDE) * 2 + lax.rem(c + dc, 2)
        )

    first = lambda k: (k * (1 - c) * SIDE + k * c) * 2
    second = lambda k: (k * c * SIDE + k * (1 - c)) * 2
    first_at = lambda k: at(k * (1 - c), k * c, 0)
    second_at = lambda k: at(k * c, k * (1 - c), 0)
    partner = at(0, 0, 1)
    near_first = (1, 3, 2)

    class Gather:
        def __init__(self, buffer, send, recv, cuts):
            self.buffer, self.send, self.recv, self.cuts = buffer, send, recv, cuts
            self.height = buffer.shape[1] // cuts
            self.sent = []

        def ref(self, slot, h):
            return self.buffer.at[slot, pl.ds(h * self.height, self.height)]

        def go(self, source, target, h, index):
            copy = remote(
                self.ref(source, h),
                self.ref(target, h),
                self.send.at[len(self.sent)],
                self.recv.at[target * self.cuts + h],
                "feat",
                index,
            )
            copy.start()
            self.sent.append(copy)

        def got(self, slot, h):
            ref = self.ref(slot, h)
            sem = self.recv.at[slot * self.cuts + h]
            remote(ref, ref, self.send.at[0], sem, "feat", partner).wait_recv()

        def stage_one(self):
            for h in range(self.cuts):
                for k in near_first:
                    self.go(0, first(k), h, first_at(k))
            for h in range(self.cuts):
                for k in near_first:
                    self.go(0, second(k), h, second_at(k))
            for h in range(self.cuts):
                self.go(0, 1, h, partner)

        def stage_two(self):
            for h in range(self.cuts):
                for k in near_first:
                    self.got(first(k), h)
                    for j in near_first:
                        self.go(first(k), first(k) + second(j), h, second_at(j))
                    self.go(first(k), first(k) + 1, h, partner)

        def cross(self, slot):
            for h in range(self.cuts):
                self.got(slot, h)
                self.go(slot, slot + 1, h, partner)

        def take(self, slot):
            for h in range(self.cuts):
                self.got(slot, h)

        def drain(self):
            for copy in self.sent:
                copy.wait_send()

    for load in w_loads:
        load.wait()
    pl.semaphore_wait(barrier, PLANE - 1 + 8)
    w_gather = Gather(weights, w_send, w_recv, 1)
    w_gather.stage_one()
    for i, target in enumerate((lax.rem(z + 4, reps), lax.rem(z + reps - 4, reps))):
        pl.semaphore_signal(
            ready_sems.at[i], inc=1, device_id={"rep": target}, device_id_type=MESH
        )

    pltpu.make_async_copy(feats, feats, load_sems.at[2]).wait()
    for b in range(blocks):
        if b % chunk == 0:
            tile_loads[b // chunk].wait()
        used = count_ref[0, b]
        left = jnp.concatenate(
            [feats[src_ref[k, 0, b]] * (k < used).astype(F32).astype(BF16) for k in range(slots)],
            axis=1,
        )
        right = jnp.concatenate([tiles[b, k] for k in range(slots)], axis=1)
        means[b] = lax.dot_general(
            left, right, (((1,), (1,)), ((), ())), preferred_element_type=F32
        ).astype(BF16)

    def arrange(p, carry):
        block = order_ref[0, p]
        mine[p, 0:32, :] = feats[block]
        mine[p, 32:64, :] = means[block]
        return carry

    lax.fori_loop(0, PLANE, arrange, 0, unroll=4)

    w_gather.stage_two()

    def send_rows(d, carry):
        dx, dy, dc = d // (2 * SIDE), (d // 2) % SIDE, d % 2
        target = at(dx, dy, dc)
        remote(
            mine.at[target], rows.at[d], a2a_send, a2a_recv.at[d], "feat", target
        ).start()
        return carry

    lax.fori_loop(1, PLANE, send_rows, 0)
    rows[0] = mine[me]
    for load in small_loads:
        load.wait()

    for k in near_first:
        w_gather.cross(second(k))
    for k in near_first:
        for j in near_first:
            w_gather.cross(first(k) + second(j))
    for s in range(SIDE * SIDE):
        w_gather.take(2 * s + 1)

    preact = jnp.broadcast_to(bias[...], (128, 256))
    for g in (0, 1, 2, 3, 6, 7, 4, 5):
        for d in range(4 * g, 4 * g + 4):
            if d:
                remote(
                    rows.at[d], rows.at[d], a2a_send, a2a_recv.at[d], "feat", partner
                ).wait_recv()
        left = rows[4 * g : 4 * g + 4].reshape(256, 128)
        right = weights[4 * g : 4 * g + 4].reshape(256, 256)
        preact = preact + lax.dot_general(
            left, right, (((0,), (0,)), ((), ())), preferred_element_type=F32
        )
    squash = jax.nn.sigmoid(preact)
    slope = cot[...].astype(F32) * squash * (1.0 + preact * (1.0 - squash))
    grads[0] = slope.astype(BF16)
    g_gather = Gather(grads, g_send, g_recv, 2)
    g_gather.stage_one()
    hidden[...] = (preact * squash).astype(BF16)
    hidden_copy = pltpu.make_async_copy(hidden, hidden_out, out_sems.at[0])
    hidden_copy.start()

    def term(slot):
        dx, dy, dc = slot // (2 * SIDE), (slot // 2) % SIDE, slot % 2
        owner = at(SIDE - dx, SIDE - dy, dc)
        return jnp.dot(mine[owner], grads[slot], preferred_element_type=F32)

    grad = term(0)
    g_gather.stage_two()
    for k in near_first:
        grad = grad + term(first(k))
    for k in near_first:
        g_gather.cross(second(k))
        grad = grad + term(second(k))
    g_gather.take(1)
    grad = grad + term(1)
    for k in near_first:
        for j in near_first:
            g_gather.cross(first(k) + second(j))
            grad = grad + term(first(k) + second(j))
    for k in near_first:
        for side in (second(k), first(k)):
            g_gather.take(side + 1)
            grad = grad + term(side + 1)
    for k in near_first:
        for j in near_first:
            slot = second(k) + first(j) + 1
            g_gather.take(slot)
            grad = grad + term(slot)

    for row in range(8):
        for col in range(2):
            piece = row * 2 + col
            part[piece // 4, piece % 4] = grad[row * 8 : row * 8 + 8, col * 128 : col * 128 + 128]

    sent = []

    def send_rep(source, target, offset):
        copy = remote(
            source,
            target,
            z_send.at[len(sent)],
            z_recv.at[len(sent)],
            "rep",
            lax.rem(z + reps + offset, reps),
        )
        copy.start()
        sent.append(copy)

    for o in (2, 1, -1):
        send_rep(part.at[lax.rem(z + 4 + o, 4)], near.at[o % 4], o)
    for copy in sent[0:3]:
        copy.wait_recv()
    far[z // 4] = (part[lax.rem(z, 4)] + near[2]) + (near[1] + near[3])
    pl.semaphore_wait(ready_sems.at[0], 1)
    pl.semaphore_wait(ready_sems.at[1], 1)
    for o in (8, 4, -4):
        send_rep(far.at[z // 4], far.at[z // 4], o)
    for i, o in enumerate((8, 4, -4)):
        slot = far.at[lax.rem(z + reps - o, reps) // 4]
        remote(slot, slot, z_send.at[3 + i], z_recv.at[3 + i], "rep", z).wait_recv()
    whole[...] = (far[0] + far[1]) + (far[2] + far[3])
    for o in (2, 1, -1):
        send_rep(whole, total_out.at[o % 4], o)
    own = pltpu.make_async_copy(whole, total_out.at[0], out_sems.at[1])
    own.start()

    for copy in sent[0:6]:
        copy.wait_send()
    all_rows = pl.ds(1, PLANE - 1)
    remote(
        mine.at[all_rows], mine.at[all_rows], a2a_send, a2a_recv.at[0], "feat", partner
    ).wait_send()
    w_gather.drain()
    g_gather.drain()
    hidden_copy.wait()
    own.wait()
    for copy in sent[6:9]:
        copy.wait()


def finish_kernel(hidden_in, total_in, hidden_ref, grad_self_ref, grad_neigh_ref):
    z = lax.axis_index("rep")
    hidden_ref[0] = hidden_in[...]
    for piece in range(16):
        row, col = piece // 2, piece % 2
        value = total_in[lax.rem(z + 4 - piece // 4, 4), piece % 4]
        target = grad_self_ref if row < 4 else grad_neigh_ref
        target[row % 4 * 8 : row % 4 * 8 + 8, col * 128 : col * 128 + 128] = value


def solution(mesh):
    reps = mesh.shape["rep"]

    def body(feats, w_self, w_neigh, bias, tile_weight, tile_src, tile_count, owner_order, cotangent):
        slots = tile_weight.shape[2]
        smem = pl.BlockSpec(memory_space=pltpu.SMEM)
        vmem = pl.BlockSpec(memory_space=pltpu.VMEM)
        anywhere = pl.BlockSpec(memory_space=pl.ANY)
        dma = pltpu.SemaphoreType.DMA
        hidden, total = pl.pallas_call(
            functools.partial(exchange_kernel, reps, slots),
            out_shape=(
                jax.ShapeDtypeStruct((128, 256), BF16),
                jax.ShapeDtypeStruct((4, 4, 8, 128), F32),
            ),
            in_specs=[smem] * 3 + [anywhere] * 6,
            out_specs=(anywhere, anywhere),
            scratch_shapes=[
                pltpu.VMEM((64, 32, 128), BF16),
                pltpu.VMEM((32, slots, 128, 128), BF16),
                pltpu.VMEM((32, 32, 128), BF16),
                pltpu.VMEM((PLANE, 64, 128), BF16),
                pltpu.VMEM((PLANE, 64, 128), BF16),
                pltpu.VMEM((PLANE, 64, 256), BF16),
                pltpu.VMEM((PLANE, 128, 256), BF16),
                pltpu.VMEM((128, 256), BF16),
                pltpu.VMEM((1, 256), F32),
                pltpu.VMEM((128, 256), BF16),
                pltpu.VMEM((4, 4, 8, 128), F32),
                pltpu.VMEM((4, 4, 8, 128), F32),
                pltpu.VMEM((4, 4, 8, 128), F32),
                pltpu.VMEM((4, 8, 128), F32),
                dma((5,)),
                dma((8,)),
                dma((2,)),
                pltpu.SemaphoreType.REGULAR((2,)),
                dma,
                dma((PLANE,)),
                dma((PLANE,)),
                dma((PLANE,)),
                dma((2 * PLANE,)),
                dma((2 * PLANE,)),
                dma((9,)),
                dma((9,)),
            ],
            compiler_params=pltpu.CompilerParams(collective_id=0, has_side_effects=True),
            name="exchange",
        )(
            tile_src.transpose(2, 0, 1),
            tile_count,
            owner_order,
            feats[0].T,
            tile_weight[0],
            w_self,
            w_neigh,
            bias.reshape(1, -1),
            cotangent[0],
        )
        return pl.pallas_call(
            finish_kernel,
            out_shape=(
                jax.ShapeDtypeStruct((1, 128, 256), BF16),
                jax.ShapeDtypeStruct((32, 256), F32),
                jax.ShapeDtypeStruct((32, 256), F32),
            ),
            in_specs=[vmem] * 2,
            out_specs=(vmem,) * 3,
            name="finish",
        )(hidden, total)

    in_specs = (
        P("rep", None, "feat"),
        P("feat", None),
        P("feat", None),
        P(),
        P("rep", None, None, None, None),
        P("rep", None, None),
        P("rep", None),
        P("rep", None),
        P("rep", "feat", None),
    )
    out_specs = (P("rep", "feat", None), P("feat", None), P("feat", None))
    return jax.shard_map(body, mesh=mesh, in_specs=in_specs, out_specs=out_specs, check_vma=False)
```

time: 68.9 us -> 60.8 us (0.88)
  Pallas kernels: 66.7 us -> 60 us
  local copies, waits for them, and re-layouts: 1.26 us -> 0 us
    pallas_call x1, Pallas kernels: 65.2 us -> 58.4 us  [body(): pl.pallas_call(functools.partial(exchange_kernel, reps, slots), out_shape...]
    unnamed x1 -> x0, local copies, waits for them, and re-layouts: 1.26 us -> none
where the time goes in v2:
time: 60.8 us; the launch traced here: 60.6 us
  Pallas kernels  60 us (99%)
  between operations  0.64 us (1%)
    pallas_call x1, Pallas kernels, body(): pl.pallas_call(functools.partial(exchange_kernel, reps, slots), out_shape...  58.4 us
    pallas_call x1, Pallas kernels, body(): pl.pallas_call(finish_kernel, out_shape=(jax.ShapeDtypeStruct((1, 128, 25...  1.52 us

profile of v2, /device:TPU:1, one launch (start us, length us, event | category | flops | bytes accessed | tf_op | source)
XLA Modules:
  0.0 60.6 jit_solution(14986021623512183507)
XLA Ops:
  0.6 58.4 %exchange.1 = (bf16[128,256]{1,0:T(8,128)(2,1)}, f32[4,4,8,128]{3,2,1,0:T(8,128)}) custom-call(s32[3,1,32]{2,1,0:T(1,128)} %bitcast.10, s32[1,32]{1,0:T(1,128)} %count_ref.1, s32[1,32]{1,0:T(1,128)} %order_ref.1, bf16[32,8192]{1,0:T(8,128)(2,1)} %bitcast.8, bf16[32,3,128,128]{3,2,1,0:T(8,128)(2,1)} %bitcast.7, bf16[32,256]{1,0:T(8,128)(2,1)} %w_self_hbm.1, ...), custom_call_target="tpu_custom_call" | custom-call | tf_op jit(solution)/shard_map/exchange/pallas_call | solution.py:357
  59.1 1.5 %finish.1 = (bf16[1,128,256]{2,1,0:T(8,128)(2,1)}, f32[32,256]{1,0:T(8,128)}, f32[32,256]{1,0:T(8,128)}) custom-call(bf16[128,256]{1,0:T(8,128)(2,1)} %get-tuple-element.5.hidden_in, f32[4,4,8,128]{3,2,1,0:T(8,128)} %get-tuple-element.6.total_in), custom_call_target="tpu_custom_call" | custom-call | tf_op jit(solution)/shard_map/finish/pallas_call | solution.py:406

commit v3 on v2

--- a/solution.py
+++ b/solution.py
@@ -28,9 +28,9 @@
 def exchange_kernel(
     reps,
     slots,
-    src_ref,
-    count_ref,
-    order_ref,
+    src_hbm,
+    count_hbm,
+    order_hbm,
     feats_hbm,
     tiles_hbm,
     w_self_hbm,
@@ -39,6 +39,9 @@
     cot_hbm,
     hidden_out,
     total_out,
+    src_ref,
+    count_ref,
+    order_ref,
     feats,
     tiles,
     means,
@@ -75,17 +78,35 @@
 
     barrier = pltpu.get_barrier_semaphore()
 
-    def greet_plane(d, carry):
-        pl.semaphore_signal(
-            barrier, inc=1, device_id={"feat": lax.rem(me + d, PLANE)}, device_id_type=MESH
-        )
-        return carry
-
-    lax.fori_loop(1, PLANE, greet_plane, 0)
-    for d in range(1, 5):
-        for target in (lax.rem(z + d, reps), lax.rem(z + reps - d, reps)):
-            pl.semaphore_signal(barrier, inc=1, device_id={"rep": target}, device_id_type=MESH)
-
+    at_x = [lax.rem(x + d, SIDE) * (2 * SIDE) for d in range(SIDE)]
+    at_y = [lax.rem(y + d, SIDE) * 2 for d in range(SIDE)]
+    at_c = [c, 1 - c]
+    at = lambda dx, dy, dc: at_x[dx % SIDE] + at_y[dy % SIDE] + at_c[dc]
+    first = lambda k: (k * (1 - c) * SIDE + k * c) * 2
+    second = lambda k: (k * c * SIDE + k * (1 - c)) * 2
+    first_at = lambda k: at(k, 0, 0) * (1 - c) + at(0, k, 0) * c
+    second_at = lambda k: at(k, 0, 0) * c + at(0, k, 0) * (1 - c)
+    partner = at(0, 0, 1)
+    near_first = (1, 3, 2)
+    along = lambda o: lax.rem(z + reps + o, reps)
+
+    def signal(sem, axis, index):
+        pl.semaphore_signal(sem, inc=1, device_id={axis: index}, device_id_type=MESH)
+
+    for k in near_first:
+        signal(barrier, "feat", at(k, 0, 0))
+        signal(barrier, "feat", at(0, k, 0))
+    signal(barrier, "feat", partner)
+    for o in (1, -1, 2, -2):
+        signal(barrier, "rep", along(o))
+
+    index_loads = [
+        pltpu.make_async_copy(src_hbm, src_ref, load_sems.at[5]),
+        pltpu.make_async_copy(count_hbm, count_ref, load_sems.at[6]),
+        pltpu.make_async_copy(order_hbm, order_ref, load_sems.at[7]),
+    ]
+    for load in index_loads:
+        load.start()
     w_loads = [
         pltpu.make_async_copy(w_self_hbm, weights.at[0, pl.ds(0, 32)], load_sems.at[0]),
         pltpu.make_async_copy(w_neigh_hbm, weights.at[0, pl.ds(32, 32)], load_sems.at[1]),
@@ -111,18 +132,6 @@
     for load in small_loads:
         load.start()
 
-    def at(dx, dy, dc):
-        return (
-            lax.rem(x + dx, SIDE) * (2 * SIDE) + lax.rem(y + dy, SIDE) * 2 + lax.rem(c + dc, 2)
-        )
-
-    first = lambda k: (k * (1 - c) * SIDE + k * c) * 2
-    second = lambda k: (k * c * SIDE + k * (1 - c)) * 2
-    first_at = lambda k: at(k * (1 - c), k * c, 0)
-    second_at = lambda k: at(k * c, k * (1 - c), 0)
-    partner = at(0, 0, 1)
-    near_first = (1, 3, 2)
-
     class Gather:
         def __init__(self, buffer, send, recv, cuts):
             self.buffer, self.send, self.recv, self.cuts = buffer, send, recv, cuts
@@ -159,18 +168,15 @@
             for h in range(self.cuts):
                 self.go(0, 1, h, partner)
 
-        def stage_two(self):
-            for h in range(self.cuts):
-                for k in near_first:
-                    self.got(first(k), h)
-                    for j in near_first:
-                        self.go(first(k), first(k) + second(j), h, second_at(j))
-                    self.go(first(k), first(k) + 1, h, partner)
-
-        def cross(self, slot):
-            for h in range(self.cuts):
-                self.got(slot, h)
-                self.go(slot, slot + 1, h, partner)
+        def forward(self, k, h):
+            self.got(first(k), h)
+            for j in near_first:
+                self.go(first(k), first(k) + second(j), h, second_at(j))
+            self.go(first(k), first(k) + 1, h, partner)
+
+        def cross(self, slot, h):
+            self.got(slot, h)
+            self.go(slot, slot + 1, h, partner)
 
         def take(self, slot):
             for h in range(self.cuts):
@@ -182,18 +188,29 @@
 
     for load in w_loads:
         load.wait()
-    pl.semaphore_wait(barrier, PLANE - 1 + 8)
+    pl.semaphore_wait(barrier, 11)
     w_gather = Gather(weights, w_send, w_recv, 1)
     w_gather.stage_one()
-    for i, target in enumerate((lax.rem(z + 4, reps), lax.rem(z + reps - 4, reps))):
-        pl.semaphore_signal(
-            ready_sems.at[i], inc=1, device_id={"rep": target}, device_id_type=MESH
-        )
-
+    for k in near_first:
+        signal(ready_sems.at[k], "feat", first_at(k))
+    signal(ready_sems.at[4], "rep", along(2))
+    signal(ready_sems.at[5], "rep", along(-2))
+
+    def pass_on():
+        for i in (1, 3, 2, 4, 5):
+            pl.semaphore_wait(ready_sems.at[i], 1)
+        signal(ready_sems.at[0], "feat", partner)
+        signal(ready_sems.at[6], "rep", along(4))
+        signal(ready_sems.at[7], "rep", along(-4))
+
+    for load in index_loads:
+        load.wait()
     pltpu.make_async_copy(feats, feats, load_sems.at[2]).wait()
     for b in range(blocks):
         if b % chunk == 0:
             tile_loads[b // chunk].wait()
+        if b == blocks - chunk:
+            pass_on()
         used = count_ref[0, b]
         left = jnp.concatenate(
             [feats[src_ref[k, 0, b]] * (k < used).astype(F32).astype(BF16) for k in range(slots)],
@@ -212,26 +229,24 @@
 
     lax.fori_loop(0, PLANE, arrange, 0, unroll=4)
 
-    w_gather.stage_two()
-
-    def send_rows(d, carry):
-        dx, dy, dc = d // (2 * SIDE), (d // 2) % SIDE, d % 2
-        target = at(dx, dy, dc)
+    pl.semaphore_wait(ready_sems.at[0], 1)
+    w_gather.forward(1, 0)
+    w_gather.forward(3, 0)
+    for d in list(range(16, 24)) + list(range(8, 16)) + list(range(24, 32)) + list(range(1, 8)):
+        target = at(d // (2 * SIDE), d // 2 % SIDE, d % 2)
         remote(
             mine.at[target], rows.at[d], a2a_send, a2a_recv.at[d], "feat", target
         ).start()
-        return carry
-
-    lax.fori_loop(1, PLANE, send_rows, 0)
+    w_gather.forward(2, 0)
     rows[0] = mine[me]
     for load in small_loads:
         load.wait()
 
     for k in near_first:
-        w_gather.cross(second(k))
+        w_gather.cross(second(k), 0)
     for k in near_first:
         for j in near_first:
-            w_gather.cross(first(k) + second(j))
+            w_gather.cross(first(k) + second(j), 0)
     for s in range(SIDE * SIDE):
         w_gather.take(2 * s + 1)
 
@@ -256,33 +271,44 @@
     hidden_copy = pltpu.make_async_copy(hidden, hidden_out, out_sems.at[0])
     hidden_copy.start()
 
-    def term(slot):
-        dx, dy, dc = slot // (2 * SIDE), (slot // 2) % SIDE, slot % 2
-        owner = at(SIDE - dx, SIDE - dy, dc)
-        return jnp.dot(mine[owner], grads[slot], preferred_element_type=F32)
-
-    grad = term(0)
-    g_gather.stage_two()
-    for k in near_first:
-        grad = grad + term(first(k))
-    for k in near_first:
-        g_gather.cross(second(k))
-        grad = grad + term(second(k))
+    def owner(slot):
+        dx, dy, dc = slot // (2 * SIDE), lax.rem(slot // 2, SIDE), lax.rem(slot, 2)
+        return (
+            lax.rem(x + SIDE - dx, SIDE) * (2 * SIDE)
+            + lax.rem(y + SIDE - dy, SIDE) * 2
+            + lax.rem(c + dc, 2)
+        )
+
+    def terms(group):
+        result = jnp.zeros((64, 256), F32)
+        for i in range(0, len(group), 2):
+            pair = group[i : i + 2]
+            left = jnp.concatenate([mine[owner(slot)] for slot in pair], axis=1)
+            right = jnp.concatenate([grads[slot] for slot in pair], axis=0)
+            result = result + jnp.dot(left, right, preferred_element_type=F32)
+        return result
+
+    corners = [(k, j) for k in near_first for j in near_first]
+    for h in range(2):
+        for k in near_first:
+            g_gather.forward(k, h)
+    for h in range(2):
+        for k in near_first:
+            g_gather.cross(second(k), h)
+    straight = [side(k) for k in near_first for side in (first, second)]
+    grad = terms([jnp.int32(0)] + straight)
     g_gather.take(1)
-    grad = grad + term(1)
-    for k in near_first:
-        for j in near_first:
-            g_gather.cross(first(k) + second(j))
-            grad = grad + term(first(k) + second(j))
-    for k in near_first:
-        for side in (second(k), first(k)):
-            g_gather.take(side + 1)
-            grad = grad + term(side + 1)
-    for k in near_first:
-        for j in near_first:
-            slot = second(k) + first(j) + 1
-            g_gather.take(slot)
-            grad = grad + term(slot)
+    for slot in straight:
+        g_gather.take(slot + 1)
+    grad = grad + terms([jnp.int32(1)] + [slot + 1 for slot in straight])
+    for h in range(2):
+        for k, j in corners:
+            g_gather.cross(first(k) + second(j), h)
+    grad = grad + terms([first(k) + second(j) for k, j in corners])
+    last = [second(k) + first(j) + 1 for k, j in corners]
+    for slot in last:
+        g_gather.take(slot)
+    grad = grad + terms(last)
 
     for row in range(8):
         for col in range(2):
@@ -308,8 +334,8 @@
     for copy in sent[0:3]:
         copy.wait_recv()
     far[z // 4] = (part[lax.rem(z, 4)] + near[2]) + (near[1] + near[3])
-    pl.semaphore_wait(ready_sems.at[0], 1)
-    pl.semaphore_wait(ready_sems.at[1], 1)
+    pl.semaphore_wait(ready_sems.at[6], 1)
+    pl.semaphore_wait(ready_sems.at[7], 1)
     for o in (8, 4, -4):
         send_rep(far.at[z // 4], far.at[z // 4], o)
     for i, o in enumerate((8, 4, -4)):
@@ -350,7 +376,6 @@
 
     def body(feats, w_self, w_neigh, bias, tile_weight, tile_src, tile_count, owner_order, cotangent):
         slots = tile_weight.shape[2]
-        smem = pl.BlockSpec(memory_space=pltpu.SMEM)
         vmem = pl.BlockSpec(memory_space=pltpu.VMEM)
         anywhere = pl.BlockSpec(memory_space=pl.ANY)
         dma = pltpu.SemaphoreType.DMA
@@ -360,9 +385,12 @@
                 jax.ShapeDtypeStruct((128, 256), BF16),
                 jax.ShapeDtypeStruct((4, 4, 8, 128), F32),
             ),
-            in_specs=[smem] * 3 + [anywhere] * 6,
+            in_specs=[anywhere] * 9,
             out_specs=(anywhere, anywhere),
             scratch_shapes=[
+                pltpu.SMEM((slots, 1, 32), jnp.int32),
+                pltpu.SMEM((1, 32), jnp.int32),
+                pltpu.SMEM((1, 32), jnp.int32),
                 pltpu.VMEM((64, 32, 128), BF16),
                 pltpu.VMEM((32, slots, 128, 128), BF16),
                 pltpu.VMEM((32, 32, 128), BF16),
@@ -377,10 +405,10 @@
                 pltpu.VMEM((4, 4, 8, 128), F32),
                 pltpu.VMEM((4, 4, 8, 128), F32),
                 pltpu.VMEM((4, 8, 128), F32),
-                dma((5,)),
+                dma((8,)),
                 dma((8,)),
                 dma((2,)),
-                pltpu.SemaphoreType.REGULAR((2,)),
+                pltpu.SemaphoreType.REGULAR((8,)),
                 dma,
                 dma((PLANE,)),
                 dma((PLANE,)),

time: 60.8 us -> 59.1 us (0.972); the launches traced: 60.6 us -> 58.2 us
  Pallas kernels: 60 us -> 57.6 us
    pallas_call x1, Pallas kernels: 58.4 us -> 56 us  [body(): pl.pallas_call(functools.partial(exchange_kernel, reps, slots), out_shape...]
where the time goes in v3:
time: 59.1 us; the launch traced here: 58.2 us
  Pallas kernels  57.6 us (97%)
  between operations  0.64 us (1%)
    pallas_call x1, Pallas kernels, body(): pl.pallas_call(functools.partial(exchange_kernel, reps, slots), out_shape...  56 us
    pallas_call x1, Pallas kernels, body(): pl.pallas_call(finish_kernel, out_shape=(jax.ShapeDtypeStruct((1, 128, 25...  1.52 us

profile of v3, /device:TPU:1, one launch (start us, length us, event | category | flops | bytes accessed | tf_op | source)
XLA Modules:
  0.0 58.2 jit_solution(11727889622881044632)
XLA Ops:
  0.6 56.0 %exchange.1 = (bf16[128,256]{1,0:T(8,128)(2,1)}, f32[4,4,8,128]{3,2,1,0:T(8,128)}) custom-call(s32[3,1,32]{2,1,0:T(1,128)} %bitcast.10, s32[1,32]{1,0:T(1,128)} %count_hbm.1, s32[1,32]{1,0:T(1,128)} %order_hbm.1, bf16[32,8192]{1,0:T(8,128)(2,1)} %bitcast.8, bf16[32,3,128,128]{3,2,1,0:T(8,128)(2,1)} %bitcast.7, bf16[32,256]{1,0:T(8,128)(2,1)} %w_self_hbm.1, ...), custom_call_target="tpu_custom_call" | custom-call | tf_op jit(solution)/shard_map/exchange/pallas_call | solution.py:382
  56.7 1.5 %finish.1 = (bf16[1,128,256]{2,1,0:T(8,128)(2,1)}, f32[32,256]{1,0:T(8,128)}, f32[32,256]{1,0:T(8,128)}) custom-call(bf16[128,256]{1,0:T(8,128)(2,1)} %get-tuple-element.5.hidden_in, f32[4,4,8,128]{3,2,1,0:T(8,128)} %get-tuple-element.6.total_in), custom_call_target="tpu_custom_call" | custom-call | tf_op jit(solution)/shard_map/finish/pallas_call | solution.py:434

commit v4 on v3

--- a/solution.py
+++ b/solution.py
@@ -57,6 +57,7 @@
     far,
     whole,
     load_sems,
+    feat_sems,
     tile_sems,
     out_sems,
     ready_sems,
@@ -105,30 +106,32 @@
         pltpu.make_async_copy(count_hbm, count_ref, load_sems.at[6]),
         pltpu.make_async_copy(order_hbm, order_ref, load_sems.at[7]),
     ]
-    for load in index_loads:
-        load.start()
     w_loads = [
         pltpu.make_async_copy(w_self_hbm, weights.at[0, pl.ds(0, 32)], load_sems.at[0]),
         pltpu.make_async_copy(w_neigh_hbm, weights.at[0, pl.ds(32, 32)], load_sems.at[1]),
     ]
-    for load in w_loads:
-        load.start()
-
-    def load_block(s, carry):
-        lanes = pl.ds(pl.multiple_of(s * 128, 128), 128)
-        pltpu.make_async_copy(feats_hbm.at[:, lanes], feats.at[s], load_sems.at[2]).start()
-        return carry
-
-    lax.fori_loop(0, feats.shape[0], load_block, 0)
-    tile_loads = []
-    for i in range(chunks):
-        piece = pl.ds(i * chunk, chunk)
-        tile_loads.append(pltpu.make_async_copy(tiles_hbm.at[piece], tiles.at[piece], tile_sems.at[i]))
-        tile_loads[-1].start()
+    feat_loads = [
+        pltpu.make_async_copy(
+            feats_hbm.at[i], feats.at[:, pl.ds(i * 8, 8)], feat_sems.at[i]
+        )
+        for i in range(4)
+    ]
     small_loads = [
         pltpu.make_async_copy(bias_hbm, bias, load_sems.at[3]),
         pltpu.make_async_copy(cot_hbm, cot, load_sems.at[4]),
     ]
+
+    def tile_load(i):
+        piece = pl.ds(i * chunk, chunk)
+        return pltpu.make_async_copy(tiles_hbm.at[piece], tiles.at[piece], tile_sems.at[i])
+
+    for load in w_loads + index_loads:
+        load.start()
+    tile_load(0).start()
+    for load in feat_loads:
+        load.start()
+    for i in range(1, chunks):
+        tile_load(i).start()
     for load in small_loads:
         load.start()
 
@@ -196,30 +199,34 @@
     signal(ready_sems.at[4], "rep", along(2))
     signal(ready_sems.at[5], "rep", along(-2))
 
-    def pass_on():
-        for i in (1, 3, 2, 4, 5):
-            pl.semaphore_wait(ready_sems.at[i], 1)
-        signal(ready_sems.at[0], "feat", partner)
-        signal(ready_sems.at[6], "rep", along(4))
-        signal(ready_sems.at[7], "rep", along(-4))
-
-    for load in index_loads:
+    for load in index_loads + feat_loads:
         load.wait()
-    pltpu.make_async_copy(feats, feats, load_sems.at[2]).wait()
-    for b in range(blocks):
-        if b % chunk == 0:
-            tile_loads[b // chunk].wait()
-        if b == blocks - chunk:
-            pass_on()
-        used = count_ref[0, b]
-        left = jnp.concatenate(
-            [feats[src_ref[k, 0, b]] * (k < used).astype(F32).astype(BF16) for k in range(slots)],
-            axis=1,
-        )
-        right = jnp.concatenate([tiles[b, k] for k in range(slots)], axis=1)
-        means[b] = lax.dot_general(
-            left, right, (((1,), (1,)), ((), ())), preferred_element_type=F32
-        ).astype(BF16)
+
+    def combine(i, carry):
+        tile_load(i).wait()
+        for b in range(chunk):
+            block = i * chunk + b
+            used = count_ref[0, block]
+            left = jnp.concatenate(
+                [
+                    feats[src_ref[k, 0, block]] * (k < used).astype(F32).astype(BF16)
+                    for k in range(slots)
+                ],
+                axis=1,
+            )
+            right = jnp.concatenate([tiles[block, k] for k in range(slots)], axis=1)
+            means[block] = lax.dot_general(
+                left, right, (((1,), (1,)), ((), ())), preferred_element_type=F32
+            ).astype(BF16)
+        return carry
+
+    lax.fori_loop(0, chunks - 1, combine, 0)
+    for k in near_first:
+        pl.semaphore_wait(ready_sems.at[k], 1)
+    signal(ready_sems.at[0], "feat", partner)
+    for k in near_first:
+        w_gather.forward(k, 0)
+    lax.fori_loop(chunks - 1, chunks, combine, 0)
 
     def arrange(p, carry):
         block = order_ref[0, p]
@@ -230,14 +237,15 @@
     lax.fori_loop(0, PLANE, arrange, 0, unroll=4)
 
     pl.semaphore_wait(ready_sems.at[0], 1)
-    w_gather.forward(1, 0)
-    w_gather.forward(3, 0)
     for d in list(range(16, 24)) + list(range(8, 16)) + list(range(24, 32)) + list(range(1, 8)):
         target = at(d // (2 * SIDE), d // 2 % SIDE, d % 2)
         remote(
             mine.at[target], rows.at[d], a2a_send, a2a_recv.at[d], "feat", target
         ).start()
-    w_gather.forward(2, 0)
+    for i in (4, 5):
+        pl.semaphore_wait(ready_sems.at[i], 1)
+    signal(ready_sems.at[6], "rep", along(4))
+    signal(ready_sems.at[7], "rep", along(-4))
     rows[0] = mine[me]
     for load in small_loads:
         load.wait()
@@ -406,6 +414,7 @@
                 pltpu.VMEM((4, 4, 8, 128), F32),
                 pltpu.VMEM((4, 8, 128), F32),
                 dma((8,)),
+                dma((4,)),
                 dma((8,)),
                 dma((2,)),
                 pltpu.SemaphoreType.REGULAR((8,)),
@@ -424,7 +433,7 @@
             tile_src.transpose(2, 0, 1),
             tile_count,
             owner_order,
-            feats[0].T,
+            feats[0].T.reshape(4, 8, 64, 128).transpose(0, 2, 1, 3),
             tile_weight[0],
             w_self,
             w_neigh,

time: 59.1 us -> 58.8 us (level)
  no operation moved by 1% of the time
where the time goes in v4:
time: 58.8 us; the launch traced here: 58.2 us
  Pallas kernels  57.6 us (98%)
  between operations  0.64 us (1%)
    pallas_call x1, Pallas kernels, body(): pl.pallas_call(functools.partial(exchange_kernel, reps, slots), out_shape...  56 us
    pallas_call x1, Pallas kernels, body(): pl.pallas_call(finish_kernel, out_shape=(jax.ShapeDtypeStruct((1, 128, 25...  1.52 us

profile of v4, /device:TPU:1, one launch (start us, length us, event | category | flops | bytes accessed | tf_op | source)
XLA Modules:
  0.0 58.2 jit_solution(4645527386257816584)
XLA Ops:
  0.6 56.0 %exchange.1 = (bf16[128,256]{1,0:T(8,128)(2,1)}, f32[4,4,8,128]{3,2,1,0:T(8,128)}) custom-call(s32[3,1,32]{2,1,0:T(1,128)} %bitcast.14, s32[1,32]{1,0:T(1,128)} %count_hbm.1, s32[1,32]{1,0:T(1,128)} %order_hbm.1, bf16[4,64,8,128]{3,2,1,0:T(8,128)(2,1)} %bitcast.12, bf16[32,3,128,128]{3,2,1,0:T(8,128)(2,1)} %bitcast.11, bf16[32,256]{1,0:T(8,128)(2,1)} %w_self_hbm.1, ...), custom_call_target="tpu_custom_call" | custom-call | tf_op jit(solution)/shard_map/exchange/pallas_call | solution.py:390
  56.7 1.5 %finish.1 = (bf16[1,128,256]{2,1,0:T(8,128)(2,1)}, f32[32,256]{1,0:T(8,128)}, f32[32,256]{1,0:T(8,128)}) custom-call(bf16[128,256]{1,0:T(8,128)(2,1)} %get-tuple-element.5.hidden_in, f32[4,4,8,128]{3,2,1,0:T(8,128)} %get-tuple-element.6.total_in), custom_call_target="tpu_custom_call" | custom-call | tf_op jit(solution)/shard_map/finish/pallas_call | solution.py:443

commit v5 on v4

--- a/solution.py
+++ b/solution.py
@@ -220,28 +220,50 @@
             ).astype(BF16)
         return carry
 
-    lax.fori_loop(0, chunks - 1, combine, 0)
+    peers = [
+        (dx, dy, dc)
+        for dy, dc in ((2, 0), (1, 1), (3, 0), (0, 1), (2, 1), (1, 0), (3, 1), (0, 0))
+        for dx in (2, 1, 3, 0)
+        if (dx, dy, dc) != (0, 0, 0)
+    ]
+
+    def row_copy(part, source, d, target):
+        half = pl.ds(part * 32, 32)
+        return remote(
+            mine.at[source, half],
+            rows.at[d, half],
+            a2a_send.at[part],
+            a2a_recv.at[part, d],
+            "feat",
+            target,
+        )
+
+    def send_rows(part):
+        for dx, dy, dc in peers:
+            target = at(dx, dy, dc)
+            row_copy(part, target, (dx * SIDE + dy) * 2 + dc, target).start()
+
+    def arrange_rows(p, carry):
+        mine[p, 0:32, :] = feats[order_ref[0, p]]
+        return carry
+
+    def arrange_means(p, carry):
+        mine[p, 32:64, :] = means[order_ref[0, p]]
+        return carry
+
+    lax.fori_loop(0, PLANE, arrange_rows, 0, unroll=8)
+    lax.fori_loop(0, 4, combine, 0)
     for k in near_first:
         pl.semaphore_wait(ready_sems.at[k], 1)
     signal(ready_sems.at[0], "feat", partner)
+    lax.fori_loop(4, 6, combine, 0)
+    pl.semaphore_wait(ready_sems.at[0], 1)
+    send_rows(0)
+    lax.fori_loop(6, chunks, combine, 0)
+    lax.fori_loop(0, PLANE, arrange_means, 0, unroll=8)
     for k in near_first:
         w_gather.forward(k, 0)
-    lax.fori_loop(chunks - 1, chunks, combine, 0)
-
-    def arrange(p, carry):
-        block = order_ref[0, p]
-        mine[p, 0:32, :] = feats[block]
-        mine[p, 32:64, :] = means[block]
-        return carry
-
-    lax.fori_loop(0, PLANE, arrange, 0, unroll=4)
-
-    pl.semaphore_wait(ready_sems.at[0], 1)
-    for d in list(range(16, 24)) + list(range(8, 16)) + list(range(24, 32)) + list(range(1, 8)):
-        target = at(d // (2 * SIDE), d // 2 % SIDE, d % 2)
-        remote(
-            mine.at[target], rows.at[d], a2a_send, a2a_recv.at[d], "feat", target
-        ).start()
+    send_rows(1)
     for i in (4, 5):
         pl.semaphore_wait(ready_sems.at[i], 1)
     signal(ready_sems.at[6], "rep", along(4))
@@ -262,9 +284,8 @@
     for g in (0, 1, 2, 3, 6, 7, 4, 5):
         for d in range(4 * g, 4 * g + 4):
             if d:
-                remote(
-                    rows.at[d], rows.at[d], a2a_send, a2a_recv.at[d], "feat", partner
-                ).wait_recv()
+                row_copy(0, 0, d, partner).wait_recv()
+                row_copy(1, 0, d, partner).wait_recv()
         left = rows[4 * g : 4 * g + 4].reshape(256, 128)
         right = weights[4 * g : 4 * g + 4].reshape(256, 256)
         preact = preact + lax.dot_general(
@@ -357,10 +378,11 @@
 
     for copy in sent[0:6]:
         copy.wait_send()
-    all_rows = pl.ds(1, PLANE - 1)
-    remote(
-        mine.at[all_rows], mine.at[all_rows], a2a_send, a2a_recv.at[0], "feat", partner
-    ).wait_send()
+    for part in range(2):
+        sent_rows = mine.at[pl.ds(1, PLANE - 1), pl.ds(part * 32, 32)]
+        remote(
+            sent_rows, sent_rows, a2a_send.at[part], a2a_recv.at[part, 0], "feat", partner
+        ).wait_send()
     w_gather.drain()
     g_gather.drain()
     hidden_copy.wait()
@@ -418,8 +440,8 @@
                 dma((8,)),
                 dma((2,)),
                 pltpu.SemaphoreType.REGULAR((8,)),
-                dma,
-                dma((PLANE,)),
+                dma((2,)),
+                dma((2, PLANE)),
                 dma((PLANE,)),
                 dma((PLANE,)),
                 dma((2 * PLANE,)),

time: 58.8 us -> 59.4 us (1.010)
  Pallas kernels: 57.6 us -> 58.6 us
    pallas_call x1, Pallas kernels: 56 us -> 57.1 us  [body(): pl.pallas_call(functools.partial(exchange_kernel, reps, slots), out_shape...]
where the time goes in v5:
time: 59.4 us; the launch traced here: 59.2 us
  Pallas kernels  58.6 us (99%)
  between operations  0.64 us (1%)
    pallas_call x1, Pallas kernels, body(): pl.pallas_call(functools.partial(exchange_kernel, reps, slots), out_shape...  57.1 us
    pallas_call x1, Pallas kernels, body(): pl.pallas_call(finish_kernel, out_shape=(jax.ShapeDtypeStruct((1, 128, 25...  1.52 us

profile of v5, /device:TPU:1, one launch (start us, length us, event | category | flops | bytes accessed | tf_op | source)
XLA Modules:
  0.0 59.2 jit_solution(8222514214002360852)
XLA Ops:
  0.6 57.1 %exchange.1 = (bf16[128,256]{1,0:T(8,128)(2,1)}, f32[4,4,8,128]{3,2,1,0:T(8,128)}) custom-call(s32[3,1,32]{2,1,0:T(1,128)} %bitcast.14, s32[1,32]{1,0:T(1,128)} %count_hbm.1, s32[1,32]{1,0:T(1,128)} %order_hbm.1, bf16[4,64,8,128]{3,2,1,0:T(8,128)(2,1)} %bitcast.12, bf16[32,3,128,128]{3,2,1,0:T(8,128)(2,1)} %bitcast.11, bf16[32,256]{1,0:T(8,128)(2,1)} %w_self_hbm.1, ...), custom_call_target="tpu_custom_call" | custom-call | tf_op jit(solution)/shard_map/exchange/pallas_call | solution.py:412
  57.7 1.5 %finish.1 = (bf16[1,128,256]{2,1,0:T(8,128)(2,1)}, f32[32,256]{1,0:T(8,128)}, f32[32,256]{1,0:T(8,128)}) custom-call(bf16[128,256]{1,0:T(8,128)(2,1)} %get-tuple-element.5.hidden_in, f32[4,4,8,128]{3,2,1,0:T(8,128)} %get-tuple-element.6.total_in), custom_call_target="tpu_custom_call" | custom-call | tf_op jit(solution)/shard_map/finish/pallas_call | solution.py:465

commit v6 on v4

--- a/solution.py
+++ b/solution.py
@@ -10,6 +10,7 @@
 MESH = pl.DeviceIdType.MESH
 SIDE = 4
 PLANE = 2 * SIDE * SIDE
+STEP = (0, 1, 3, 2)
 F32 = jnp.float32
 BF16 = jnp.bfloat16
 
@@ -82,19 +83,18 @@
     at_x = [lax.rem(x + d, SIDE) * (2 * SIDE) for d in range(SIDE)]
     at_y = [lax.rem(y + d, SIDE) * 2 for d in range(SIDE)]
     at_c = [c, 1 - c]
-    at = lambda dx, dy, dc: at_x[dx % SIDE] + at_y[dy % SIDE] + at_c[dc]
-    first = lambda k: (k * (1 - c) * SIDE + k * c) * 2
-    second = lambda k: (k * c * SIDE + k * (1 - c)) * 2
-    first_at = lambda k: at(k, 0, 0) * (1 - c) + at(0, k, 0) * c
-    second_at = lambda k: at(k, 0, 0) * c + at(0, k, 0) * (1 - c)
+    at_a = [at_x[d] * (1 - c) + at_y[d] * c for d in STEP]
+    at_b = [at_x[d] * c + at_y[d] * (1 - c) for d in STEP]
+    from_a = [at_x[-d % SIDE] * (1 - c) + at_y[-d % SIDE] * c for d in STEP]
+    from_b = [at_x[-d % SIDE] * c + at_y[-d % SIDE] * (1 - c) for d in STEP]
+    at = lambda a, b, dc: at_a[a] + at_b[b] + at_c[dc]
     partner = at(0, 0, 1)
-    near_first = (1, 3, 2)
     along = lambda o: lax.rem(z + reps + o, reps)
 
     def signal(sem, axis, index):
         pl.semaphore_signal(sem, inc=1, device_id={axis: index}, device_id_type=MESH)
 
-    for k in near_first:
+    for k in (1, 2, 3):
         signal(barrier, "feat", at(k, 0, 0))
         signal(barrier, "feat", at(0, k, 0))
     signal(barrier, "feat", partner)
@@ -136,54 +136,37 @@
         load.start()
 
     class Gather:
-        def __init__(self, buffer, send, recv, cuts):
-            self.buffer, self.send, self.recv, self.cuts = buffer, send, recv, cuts
-            self.height = buffer.shape[1] // cuts
-            self.sent = []
-
-        def ref(self, slot, h):
-            return self.buffer.at[slot, pl.ds(h * self.height, self.height)]
-
-        def go(self, source, target, h, index):
+        def __init__(self, buffer, send, recv):
+            self.buffer, self.send, self.recv = buffer, send, recv
+            self.sent, self.spans = [], {}
+
+        def go(self, source, count, target, index):
             copy = remote(
-                self.ref(source, h),
-                self.ref(target, h),
+                self.buffer.at[pl.ds(source, count)],
+                self.buffer.at[pl.ds(target, count)],
                 self.send.at[len(self.sent)],
-                self.recv.at[target * self.cuts + h],
+                self.recv.at[len(self.sent)],
                 "feat",
                 index,
             )
             copy.start()
+            self.spans[target] = len(self.sent)
             self.sent.append(copy)
 
-        def got(self, slot, h):
-            ref = self.ref(slot, h)
-            sem = self.recv.at[slot * self.cuts + h]
-            remote(ref, ref, self.send.at[0], sem, "feat", partner).wait_recv()
-
-        def stage_one(self):
-            for h in range(self.cuts):
-                for k in near_first:
-                    self.go(0, first(k), h, first_at(k))
-            for h in range(self.cuts):
-                for k in near_first:
-                    self.go(0, second(k), h, second_at(k))
-            for h in range(self.cuts):
-                self.go(0, 1, h, partner)
-
-        def forward(self, k, h):
-            self.got(first(k), h)
-            for j in near_first:
-                self.go(first(k), first(k) + second(j), h, second_at(j))
-            self.go(first(k), first(k) + 1, h, partner)
-
-        def cross(self, slot, h):
-            self.got(slot, h)
-            self.go(slot, slot + 1, h, partner)
-
-        def take(self, slot):
-            for h in range(self.cuts):
-                self.got(slot, h)
+        def got(self, *targets):
+            for target in targets:
+                self.sent[self.spans[target]].wait_recv()
+
+        def along_a(self):
+            for a in (1, 2, 3):
+                self.go(0, 1, a, at(a, 0, 0))
+
+        def along_b(self, first, count):
+            for b in (1, 2, 3):
+                self.go(first, count, 4 * b + first, at(0, b, 0))
+
+        def cross(self, first, count):
+            self.go(first, count, 16 + first, partner)
 
         def drain(self):
             for copy in self.sent:
@@ -192,10 +175,10 @@
     for load in w_loads:
         load.wait()
     pl.semaphore_wait(barrier, 11)
-    w_gather = Gather(weights, w_send, w_recv, 1)
-    w_gather.stage_one()
-    for k in near_first:
-        signal(ready_sems.at[k], "feat", first_at(k))
+    w_gather = Gather(weights, w_send, w_recv)
+    w_gather.along_a()
+    for k in (1, 2, 3):
+        signal(ready_sems.at[k], "feat", at(k, 0, 0))
     signal(ready_sems.at[4], "rep", along(2))
     signal(ready_sems.at[5], "rep", along(-2))
 
@@ -221,11 +204,12 @@
         return carry
 
     lax.fori_loop(0, chunks - 1, combine, 0)
-    for k in near_first:
+    for k in (1, 2, 3):
         pl.semaphore_wait(ready_sems.at[k], 1)
     signal(ready_sems.at[0], "feat", partner)
-    for k in near_first:
-        w_gather.forward(k, 0)
+    w_gather.got(1, 2, 3)
+    w_gather.along_b(0, 4)
+    w_gather.cross(0, 4)
     lax.fori_loop(chunks - 1, chunks, combine, 0)
 
     def arrange(p, carry):
@@ -237,11 +221,15 @@
     lax.fori_loop(0, PLANE, arrange, 0, unroll=4)
 
     pl.semaphore_wait(ready_sems.at[0], 1)
-    for d in list(range(16, 24)) + list(range(8, 16)) + list(range(24, 32)) + list(range(1, 8)):
-        target = at(d // (2 * SIDE), d // 2 % SIDE, d % 2)
-        remote(
-            mine.at[target], rows.at[d], a2a_send, a2a_recv.at[d], "feat", target
-        ).start()
+    for dc in range(2):
+        for b in range(SIDE):
+            for a in range(SIDE):
+                slot = 16 * dc + 4 * b + a
+                if slot:
+                    target = at(a, b, dc)
+                    remote(
+                        mine.at[target], rows.at[slot], a2a_send, a2a_recv.at[slot], "feat", target
+                    ).start()
     for i in (4, 5):
         pl.semaphore_wait(ready_sems.at[i], 1)
     signal(ready_sems.at[6], "rep", along(4))
@@ -250,16 +238,13 @@
     for load in small_loads:
         load.wait()
 
-    for k in near_first:
-        w_gather.cross(second(k), 0)
-    for k in near_first:
-        for j in near_first:
-            w_gather.cross(first(k) + second(j), 0)
-    for s in range(SIDE * SIDE):
-        w_gather.take(2 * s + 1)
-
+    for b in (1, 2, 3):
+        w_gather.got(4 * b)
+        w_gather.cross(4 * b, 4)
     preact = jnp.broadcast_to(bias[...], (128, 256))
-    for g in (0, 1, 2, 3, 6, 7, 4, 5):
+    for g in range(8):
+        if g >= 4:
+            w_gather.got(4 * g)
         for d in range(4 * g, 4 * g + 4):
             if d:
                 remote(
@@ -273,19 +258,16 @@
     squash = jax.nn.sigmoid(preact)
     slope = cot[...].astype(F32) * squash * (1.0 + preact * (1.0 - squash))
     grads[0] = slope.astype(BF16)
-    g_gather = Gather(grads, g_send, g_recv, 2)
-    g_gather.stage_one()
+    g_gather = Gather(grads, g_send, g_recv)
+    g_gather.along_a()
+    g_gather.along_b(0, 1)
     hidden[...] = (preact * squash).astype(BF16)
     hidden_copy = pltpu.make_async_copy(hidden, hidden_out, out_sems.at[0])
     hidden_copy.start()
 
     def owner(slot):
-        dx, dy, dc = slot // (2 * SIDE), lax.rem(slot // 2, SIDE), lax.rem(slot, 2)
-        return (
-            lax.rem(x + SIDE - dx, SIDE) * (2 * SIDE)
-            + lax.rem(y + SIDE - dy, SIDE) * 2
-            + lax.rem(c + dc, 2)
-        )
+        dc, b, a = slot // 16, slot // 4 % 4, slot % 4
+        return (from_b[a] + from_a[b] if dc else from_a[a] + from_b[b]) + at_c[dc]
 
     def terms(group):
         result = jnp.zeros((64, 256), F32)
@@ -296,27 +278,24 @@
             result = result + jnp.dot(left, right, preferred_element_type=F32)
         return result
 
-    corners = [(k, j) for k in near_first for j in near_first]
-    for h in range(2):
-        for k in near_first:
-            g_gather.forward(k, h)
-    for h in range(2):
-        for k in near_first:
-            g_gather.cross(second(k), h)
-    straight = [side(k) for k in near_first for side in (first, second)]
-    grad = terms([jnp.int32(0)] + straight)
-    g_gather.take(1)
-    for slot in straight:
-        g_gather.take(slot + 1)
-    grad = grad + terms([jnp.int32(1)] + [slot + 1 for slot in straight])
-    for h in range(2):
-        for k, j in corners:
-            g_gather.cross(first(k) + second(j), h)
-    grad = grad + terms([first(k) + second(j) for k, j in corners])
-    last = [second(k) + first(j) + 1 for k, j in corners]
-    for slot in last:
-        g_gather.take(slot)
-    grad = grad + terms(last)
+    g_gather.got(1, 2)
+    g_gather.along_b(1, 2)
+    g_gather.got(3)
+    g_gather.along_b(3, 1)
+    g_gather.cross(0, 4)
+    grad = terms([0, 1, 2, 3])
+    for b in (1, 2, 3):
+        g_gather.got(4 * b, 4 * b + 1)
+        g_gather.cross(4 * b, 3)
+    grad = grad + terms([4, 5, 6, 8, 9, 10, 12, 13, 14])
+    for b in (1, 2, 3):
+        g_gather.got(4 * b + 3)
+        g_gather.cross(4 * b + 3, 1)
+    g_gather.got(16, 20, 24, 28)
+    grad = grad + terms([16, 17, 18, 19, 20, 21, 22, 24, 25, 26, 28, 29, 30])
+    grad = grad + terms([7, 11, 15])
+    g_gather.got(23, 27, 31)
+    grad = grad + terms([23, 27, 31])
 
     for row in range(8):
         for col in range(2):
@@ -420,10 +399,10 @@
                 pltpu.SemaphoreType.REGULAR((8,)),
                 dma,
                 dma((PLANE,)),
-                dma((PLANE,)),
-                dma((PLANE,)),
-                dma((2 * PLANE,)),
-                dma((2 * PLANE,)),
+                dma((10,)),
+                dma((10,)),
+                dma((19,)),
+                dma((19,)),
                 dma((9,)),
                 dma((9,)),
             ],

time: 58.8 us -> 59.5 us (1.012)
  Pallas kernels: 57.6 us -> 58.6 us
    pallas_call x1, Pallas kernels: 56 us -> 57.1 us  [body(): pl.pallas_call(functools.partial(exchange_kernel, reps, slots), out_shape...]
where the time goes in v6:
time: 59.5 us; the launch traced here: 59.2 us
  Pallas kernels  58.6 us (98%)
  between operations  0.64 us (1%)
    pallas_call x1, Pallas kernels, body(): pl.pallas_call(functools.partial(exchange_kernel, reps, slots), out_shape...  57.1 us
    pallas_call x1, Pallas kernels, body(): pl.pallas_call(finish_kernel, out_shape=(jax.ShapeDtypeStruct((1, 128, 25...  1.52 us

profile of v6, /device:TPU:1, one launch (start us, length us, event | category | flops | bytes accessed | tf_op | source)
XLA Modules:
  0.0 59.2 jit_solution(8285950501643242757)
XLA Ops:
  0.6 57.1 %exchange.1 = (bf16[128,256]{1,0:T(8,128)(2,1)}, f32[4,4,8,128]{3,2,1,0:T(8,128)}) custom-call(s32[3,1,32]{2,1,0:T(1,128)} %bitcast.14, s32[1,32]{1,0:T(1,128)} %count_hbm.1, s32[1,32]{1,0:T(1,128)} %order_hbm.1, bf16[4,64,8,128]{3,2,1,0:T(8,128)(2,1)} %bitcast.12, bf16[32,3,128,128]{3,2,1,0:T(8,128)(2,1)} %bitcast.11, bf16[32,256]{1,0:T(8,128)(2,1)} %w_self_hbm.1, ...), custom_call_target="tpu_custom_call" | custom-call | tf_op jit(solution)/shard_map/exchange/pallas_call | solution.py:369
  57.7 1.5 %finish.1 = (bf16[1,128,256]{2,1,0:T(8,128)(2,1)}, f32[32,256]{1,0:T(8,128)}, f32[32,256]{1,0:T(8,128)}) custom-call(bf16[128,256]{1,0:T(8,128)(2,1)} %get-tuple-element.5.hidden_in, f32[4,4,8,128]{3,2,1,0:T(8,128)} %get-tuple-element.6.total_in), custom_call_target="tpu_custom_call" | custom-call | tf_op jit(solution)/shard_map/finish/pallas_call | solution.py:422

commit v7 on v4

--- a/solution.py
+++ b/solution.py
@@ -52,6 +52,7 @@
     cot,
     bias,
     hidden,
+    mine_part,
     part,
     near,
     far,
@@ -321,7 +322,9 @@
     for row in range(8):
         for col in range(2):
             piece = row * 2 + col
-            part[piece // 4, piece % 4] = grad[row * 8 : row * 8 + 8, col * 128 : col * 128 + 128]
+            value = grad[row * 8 : row * 8 + 8, col * 128 : col * 128 + 128]
+            mine_part[piece // 4, piece % 4] = value
+            part[piece // 4, piece % 4] = value.astype(BF16)
 
     sent = []
 
@@ -341,7 +344,9 @@
         send_rep(part.at[lax.rem(z + 4 + o, 4)], near.at[o % 4], o)
     for copy in sent[0:3]:
         copy.wait_recv()
-    far[z // 4] = (part[lax.rem(z, 4)] + near[2]) + (near[1] + near[3])
+    wide = lambda value: value.astype(F32)
+    window = (mine_part[lax.rem(z, 4)] + wide(near[2])) + (wide(near[1]) + wide(near[3]))
+    far[z // 4] = window.astype(BF16)
     pl.semaphore_wait(ready_sems.at[6], 1)
     pl.semaphore_wait(ready_sems.at[7], 1)
     for o in (8, 4, -4):
@@ -349,7 +354,7 @@
     for i, o in enumerate((8, 4, -4)):
         slot = far.at[lax.rem(z + reps - o, reps) // 4]
         remote(slot, slot, z_send.at[3 + i], z_recv.at[3 + i], "rep", z).wait_recv()
-    whole[...] = (far[0] + far[1]) + (far[2] + far[3])
+    whole[...] = (wide(far[0]) + wide(far[1])) + (wide(far[2]) + wide(far[3]))
     for o in (2, 1, -1):
         send_rep(whole, total_out.at[o % 4], o)
     own = pltpu.make_async_copy(whole, total_out.at[0], out_sems.at[1])
@@ -410,8 +415,9 @@
                 pltpu.VMEM((1, 256), F32),
                 pltpu.VMEM((128, 256), BF16),
                 pltpu.VMEM((4, 4, 8, 128), F32),
-                pltpu.VMEM((4, 4, 8, 128), F32),
-                pltpu.VMEM((4, 4, 8, 128), F32),
+                pltpu.VMEM((4, 4, 8, 128), BF16),
+                pltpu.VMEM((4, 4, 8, 128), BF16),
+                pltpu.VMEM((4, 4, 8, 128), BF16),
                 pltpu.VMEM((4, 8, 128), F32),
                 dma((8,)),
                 dma((4,)),

time: 58.8 us -> 58.3 us (level)
  Pallas kernels: 57.6 us -> 57 us
where the time goes in v7:
time: 58.3 us; the launch traced here: 57.6 us
  Pallas kernels  57 us (98%)
  between operations  0.64 us (1%)
    pallas_call x1, Pallas kernels, body(): pl.pallas_call(functools.partial(exchange_kernel, reps, slots), out_shape...  55.5 us
    pallas_call x1, Pallas kernels, body(): pl.pallas_call(finish_kernel, out_shape=(jax.ShapeDtypeStruct((1, 128, 25...  1.52 us

profile of v7, /device:TPU:1, one launch (start us, length us, event | category | flops | bytes accessed | tf_op | source)
XLA Modules:
  0.0 57.6 jit_solution(16672047969294955279)
XLA Ops:
  0.6 55.5 %exchange.1 = (bf16[128,256]{1,0:T(8,128)(2,1)}, f32[4,4,8,128]{3,2,1,0:T(8,128)}) custom-call(s32[3,1,32]{2,1,0:T(1,128)} %bitcast.14, s32[1,32]{1,0:T(1,128)} %count_hbm.1, s32[1,32]{1,0:T(1,128)} %order_hbm.1, bf16[4,64,8,128]{3,2,1,0:T(8,128)(2,1)} %bitcast.12, bf16[32,3,128,128]{3,2,1,0:T(8,128)(2,1)} %bitcast.11, bf16[32,256]{1,0:T(8,128)(2,1)} %w_self_hbm.1, ...), custom_call_target="tpu_custom_call" | custom-call | tf_op jit(solution)/shard_map/exchange/pallas_call | solution.py:395
  56.1 1.5 %finish.1 = (bf16[1,128,256]{2,1,0:T(8,128)(2,1)}, f32[32,256]{1,0:T(8,128)}, f32[32,256]{1,0:T(8,128)}) custom-call(bf16[128,256]{1,0:T(8,128)(2,1)} %get-tuple-element.5.hidden_in, f32[4,4,8,128]{3,2,1,0:T(8,128)} %get-tuple-element.6.total_in), custom_call_target="tpu_custom_call" | custom-call | tf_op jit(solution)/shard_map/finish/pallas_call | solution.py:449

commit v8 on v7

--- a/solution.py
+++ b/solution.py
@@ -225,8 +225,6 @@
     for k in near_first:
         pl.semaphore_wait(ready_sems.at[k], 1)
     signal(ready_sems.at[0], "feat", partner)
-    for k in near_first:
-        w_gather.forward(k, 0)
     lax.fori_loop(chunks - 1, chunks, combine, 0)
 
     def arrange(p, carry):
@@ -238,11 +236,13 @@
     lax.fori_loop(0, PLANE, arrange, 0, unroll=4)
 
     pl.semaphore_wait(ready_sems.at[0], 1)
-    for d in list(range(16, 24)) + list(range(8, 16)) + list(range(24, 32)) + list(range(1, 8)):
+    for d in range(1, 32):
         target = at(d // (2 * SIDE), d // 2 % SIDE, d % 2)
         remote(
             mine.at[target], rows.at[d], a2a_send, a2a_recv.at[d], "feat", target
         ).start()
+    for k in near_first:
+        w_gather.forward(k, 0)
     for i in (4, 5):
         pl.semaphore_wait(ready_sems.at[i], 1)
     signal(ready_sems.at[6], "rep", along(4))

time: 58.3 us -> 58.1 us (level)
  no operation moved by 1% of the time
where the time goes in v8:
time: 58.1 us; the launch traced here: 57.9 us
  Pallas kernels  57.3 us (99%)
  between operations  0.64 us (1%)
    pallas_call x1, Pallas kernels, body(): pl.pallas_call(functools.partial(exchange_kernel, reps, slots), out_shape...  55.7 us
    pallas_call x1, Pallas kernels, body(): pl.pallas_call(finish_kernel, out_shape=(jax.ShapeDtypeStruct((1, 128, 25...  1.52 us

profile of v8, /device:TPU:1, one launch (start us, length us, event | category | flops | bytes accessed | tf_op | source)
XLA Modules:
  0.0 57.9 jit_solution(8586433296342999991)
XLA Ops:
  0.6 55.7 %exchange.1 = (bf16[128,256]{1,0:T(8,128)(2,1)}, f32[4,4,8,128]{3,2,1,0:T(8,128)}) custom-call(s32[3,1,32]{2,1,0:T(1,128)} %bitcast.14, s32[1,32]{1,0:T(1,128)} %count_hbm.1, s32[1,32]{1,0:T(1,128)} %order_hbm.1, bf16[4,64,8,128]{3,2,1,0:T(8,128)(2,1)} %bitcast.12, bf16[32,3,128,128]{3,2,1,0:T(8,128)(2,1)} %bitcast.11, bf16[32,256]{1,0:T(8,128)(2,1)} %w_self_hbm.1, ...), custom_call_target="tpu_custom_call" | custom-call | tf_op jit(solution)/shard_map/exchange/pallas_call | solution.py:395
  56.4 1.5 %finish.1 = (bf16[1,128,256]{2,1,0:T(8,128)(2,1)}, f32[32,256]{1,0:T(8,128)}, f32[32,256]{1,0:T(8,128)}) custom-call(bf16[128,256]{1,0:T(8,128)(2,1)} %get-tuple-element.5.hidden_in, f32[4,4,8,128]{3,2,1,0:T(8,128)} %get-tuple-element.6.total_in), custom_call_target="tpu_custom_call" | custom-call | tf_op jit(solution)/shard_map/finish/pallas_call | solution.py:449
